TPU v7x, 256 devices: a whole 4x4x8 slice. The times are simulated.
256 devices in a mesh: region: 64 (over x, z, core), level: 4 (over y).
Axes of the slice: x: 4, y: 4, z: 8, core: 2. Of those that a mesh axis runs over, the one named last changes fastest.
Arguments:
- ensemble: bfloat16 [4, 256, 262144], P('level', None, 'region'), may hold values from -6 to 6
- obs_anomaly: bfloat16 [4, 65536, 256], P('level', 'region'), may hold values from -6 to 6
- innovation: bfloat16 [4, 65536], P('level', 'region'), may hold values from -18 to 18
- obs_precision: bfloat16 [4, 65536], P('level', 'region'), may hold values from 0.019897461 to 0.29882812
- owner_region: int32 [4, 65536, 1], P('level', 'region'), may hold values from 0 to 63; in each aligned block of 1024 rows (0 to 1023, 1024 to 2047, ..., all dimensions but the last counted through in order) at most 24 rows name the same one
- neighbours: int32 [64, 3], replicated, may hold values from 0 to 63, all different within a row
Outputs:
- analysis: bfloat16 [4, 256, 262144], P('level', None, 'region')
Inputs may be any that keep to these rules, and one draw needn't show every extreme that they name: `owner_region`: among the 1024 observations of one device (aligned blocks), no region is named more than 24 times, a bound that some block reaches. `neighbours`: each row lists 3 different regions; every region is listed by some row.
All inputs are finite; a program needn't handle non-finite values.
Results may differ from a plain program's by a relative error of at most 0.0059.
Values may be sent and summed in bfloat16 or wider, within the bound.
No kernel may reach another device: no remote copies, remote signals or barrier semaphores. Data moves between devices by JAX's collectives and lax.ppermute only.
A program may use at most 64 MiB of HBM per device.

v0:
```python
import math
import jax
import jax.numpy as jnp
from jax import lax
from jax.sharding import PartitionSpec as P

NSTEPS = 4
TAPER = 0.6


def cut_along(value, dim, count):
    before, after = (value.shape[:dim], value.shape[dim + 1 :])
    return jnp.moveaxis(value.reshape(*before, count, -1, *after), dim, 0)


def sum_at_owner(value, axis, dim):
    count = lax.axis_size(axis)
    pieces = lax.all_to_all(cut_along(value, dim, count), axis, 0, 0, tiled=True)
    return jnp.sum(pieces, axis=0)


def neighbour_weights(neighbours):
    region_ids = jnp.arange(neighbours.shape[0], dtype=jnp.int32)
    weights = (region_ids[:, None] == region_ids[None, :]).astype(jnp.float32)
    for listed in range(neighbours.shape[1]):
        hit = (neighbours[:, listed][:, None] == region_ids[None, :]).astype(jnp.float32)
        weights = weights + TAPER ** (listed + 1) * hit
    return weights


def inverse_root(matrix):
    order_size = matrix.shape[0]
    identity = jnp.eye(order_size, dtype=jnp.float32)
    norm_scale = 0.5 * jnp.sqrt(jnp.sum(matrix * matrix))
    root_iter = matrix / norm_scale
    inverse_iter = identity
    for newton_step in range(NSTEPS):
        correction = 1.5 * identity - 0.5 * jnp.dot(
            inverse_iter, root_iter, precision=lax.Precision.HIGHEST
        )
        root_iter = jnp.dot(root_iter, correction, precision=lax.Precision.HIGHEST)
        inverse_iter = jnp.dot(correction, inverse_iter, precision=lax.Precision.HIGHEST)
    return inverse_iter / jnp.sqrt(norm_scale)


def analysis_weights(covariance, innovation_sum):
    order_size = covariance.shape[0]
    identity = jnp.eye(order_size, dtype=jnp.float32)
    precision_matrix = covariance + (order_size - 1.0) * identity
    root = inverse_root(precision_matrix)
    inner = jnp.dot(root, innovation_sum, precision=lax.Precision.HIGHEST)
    mean_shift = jnp.dot(root, inner, precision=lax.Precision.HIGHEST)
    return (math.sqrt(order_size - 1.0) * root + mean_shift[:, None]).astype(jnp.bfloat16)


def update_columns(column_block, transform):
    average = jnp.mean(column_block.astype(jnp.float32), axis=0)
    anomaly = (column_block.astype(jnp.float32) - average[None, :]).astype(jnp.bfloat16)
    combined = lax.dot_general(
        transform, anomaly, (((0,), (0,)), ((), ())), preferred_element_type=jnp.float32
    )
    return (combined + average[None, :]).astype(jnp.bfloat16)


def level_factor(distance, levels):
    factor = jnp.zeros(distance.shape, jnp.float32)
    for apart in range(levels):
        factor = factor + 0.5**apart * (distance == apart).astype(jnp.float32)
    return factor


def body(ensemble, obs_anomaly, innovation, obs_precision, owner_region, neighbours):
    regions = lax.axis_size("region")
    levels = lax.axis_size("level")
    my_level = lax.axis_index("level")
    members = obs_anomaly.shape[2]
    local_obs = obs_anomaly.shape[1]
    capacity = 3 * local_obs // (2 * regions)
    slot_count = (neighbours.shape[1] + 1) * capacity
    region_weight = neighbour_weights(neighbours)
    owner_ids = owner_region[0, :, 0]
    region_ids = jnp.arange(regions, dtype=jnp.int32)
    owner_table = (owner_ids[:, None] == region_ids[None, :]).astype(jnp.float32)
    dest_weight = jnp.dot(owner_table, region_weight.T, precision=lax.Precision.HIGHEST)
    live = dest_weight > 0
    position = jnp.cumsum(live.astype(jnp.int32), axis=0) - 1
    gain = (dest_weight * obs_precision[0].astype(jnp.float32)[:, None]).astype(jnp.bfloat16)
    slot_ids = jnp.arange(slot_count, dtype=jnp.int32)
    placement = jnp.logical_and(
        live.T[:, None, :], position.T[:, None, :] == slot_ids[None, :, None]
    )
    place_float = placement.astype(jnp.float32)
    send_rows = jnp.einsum(
        "rso,om->rsm",
        placement.astype(jnp.bfloat16),
        obs_anomaly[0],
        preferred_element_type=jnp.float32,
    ).astype(jnp.bfloat16)
    send_gain = jnp.einsum(
        "rso,or->rs", place_float, gain.astype(jnp.float32), precision=lax.Precision.HIGHEST
    ).astype(jnp.bfloat16)
    send_innov = jnp.einsum(
        "rso,o->rs", place_float, innovation[0].astype(jnp.float32), precision=lax.Precision.HIGHEST
    ).astype(jnp.bfloat16)
    received = (
        lax.all_to_all(send_rows, "region", split_axis=0, concat_axis=0, tiled=True),
        lax.all_to_all(send_gain, "region", split_axis=0, concat_axis=0, tiled=True),
        lax.all_to_all(send_innov, "region", split_axis=0, concat_axis=0, tiled=True),
    )
    routed_rows = received[0].reshape(-1, members)
    routed_gain = received[1].reshape(-1)
    routed_innov = received[2].reshape(-1)
    weighted = (routed_gain.astype(jnp.float32)[:, None] * routed_rows.astype(jnp.float32)).astype(
        jnp.bfloat16
    )
    own_cov = jnp.dot(weighted.T, routed_rows, preferred_element_type=jnp.float32)
    own_sum = jnp.dot(routed_innov, weighted, preferred_element_type=jnp.float32)
    stacked = jnp.tile(own_cov, (levels, 1))
    target_level = jnp.arange(members * lax.axis_size("level"), dtype=jnp.int32) // members
    factor = level_factor(jnp.abs(target_level - my_level), levels)
    covariance = sum_at_owner(factor[:, None] * stacked, "level", 0)
    level_ids = jnp.arange(levels, dtype=jnp.int32)
    sum_terms = level_factor(jnp.abs(level_ids - my_level), levels)[:, None] * own_sum[None, :]
    all_sums = lax.psum(sum_terms, "level")
    innovation_sum = lax.dynamic_index_in_dim(all_sums, my_level, 0, keepdims=False)
    transform = analysis_weights(covariance, innovation_sum)
    return update_columns(ensemble[0], transform)[None]


def solution(mesh):
    return jax.shard_map(
        body,
        mesh=mesh,
        in_specs=(
            P("level", None, "region"),
            P("level", "region", None),
            P("level", "region"),
            P("level", "region"),
            P("level", "region", None),
            P(),
        ),
        out_specs=P("level", None, "region"),
        check_vma=False,
    )
```

profile of v0, /device:TPU:2, one launch (start us, length us, event | category | flops | bytes accessed | tf_op | source)
XLA Modules:
  0.0 175.8 jit_solution(10290218327440279134)
XLA Ops:
  0.0 0.8 slice_bitcast_fusion.2
  0.8 0.7 convert_element_type.111
  1.5 1.2 fusion.32
  2.9 18.0 %reduce-window.6 = s32[64,8,128]{2,1,0:T(8,128)S(1)} reduce-window(s32[64,8,128]{2,1,0:T(8,128)S(1)} %bitcast.82, s32[]{:T(128)} %constant.70.clone.1), window={size=1x1x128 pad=0_0x0_0x127_0}, to_apply=%region_0.0 | reduce-window | flops 8323072 | bytes 524292 | tf_op jit(solution)/shard_map/reduce-window
  21.5 4.8 %fusion.5 = f32[64,1,96]{2,1,0:T(1,128)S(1)} fusion(s32[64,1024]{1,0:T(8,128)S(1)} %bitcast.84, pred[64,1024]{1,0:T(8,128)(4,1)S(1)} %get-tuple-element.6, bf16[1024,64,1]{0,1,2:T(8,128)(2,1)S(1)} %fusion.37), kind=kOutput, calls=%fused_computation.4 | convolution fusion | flops 25165824 | bytes 483328 | tf_op jit(solution)/shard_map/rso,or->rs/dot_general | solution.py:99
  26.2 0.6 copy.17
  26.9 12.0 %all-to-all-start = ((bf16[64,1,96]{2,1,0:T(2,128)(2,1)}), bf16[64,1,96]{2,1,0:T(2,128)(2,1)S(1)}, u32[]{:S(2)}, u32[]{:S(2)}) async-start(bf16[64,1,96]{2,1,0:T(2,128)(2,1)} %copy.17), calls=%async_computation | async-start | bytes 65536 | tf_op jit(solution)/shard_map/all_to_all | solution.py:107
  38.9 6.9 %fusion.21 = bf16[64,96,256]{2,1,0:T(8,128)(2,1)} fusion(s32[64,1024]{1,0:T(8,128)S(1)} %bitcast.85, pred[64,1024]{1,0:T(8,128)(4,1)S(1)} %get-tuple-element.6, bf16[1,1024,256]{2,1,0:T(8,128)(2,1)S(1)} %copy-done), kind=kOutput, calls=%fused_computation.23 | convolution fusion | flops 3235381248 | bytes 3997696 | tf_op jit(solution)/shard_map/rso,om->rsm/dot_general | solution.py:93
  45.8 1.7 all-to-all-done
  47.5 9.0 %all-to-all-start.1 = ((bf16[64,96,256]{2,1,0:T(8,128)(2,1)}), bf16[64,96,256]{2,1,0:T(8,128)(2,1)}, u32[]{:S(2)}, u32[]{:S(2)}) async-start(bf16[64,96,256]{2,1,0:T(8,128)(2,1)} %fusion.21), calls=%async_computation.1 | async-start | bytes 6291456 | tf_op jit(solution)/shard_map/all_to_all | solution.py:106
  56.5 4.7 %fusion.1 = f32[1,64,96]{2,0,1:T(1,128)S(1)} fusion(s32[64,1024]{1,0:T(8,128)S(1)} %bitcast.86, pred[64,1024]{1,0:T(8,128)(4,1)S(1)} %get-tuple-element.6, bf16[1,1024]{1,0:T(2,128)(2,1)S(1)} %copy-done.2), kind=kOutput, calls=%fused_computation.2 | convolution fusion | flops 25165824 | bytes 354304 | tf_op jit(solution)/shard_map/rso,o->rs/dot_general | solution.py:102
  61.2 0.6 copy.18
  62.2 66.1 %all-to-all-done.1 = bf16[64,96,256]{2,1,0:T(8,128)(2,1)} async-done(((bf16[64,96,256]{2,1,0:T(8,128)(2,1)}), bf16[64,96,256]{2,1,0:T(8,128)(2,1)}, u32[]{:S(2)}, u32[]{:S(2)}) %all-to-all-start.1) | async-done | bytes 3145760 | tf_op jit(solution)/shard_map/all_to_all | solution.py:106
  128.3 7.3 %all-to-all-start.3 = ((bf16[64,1,96]{2,1,0:T(2,128)(2,1)}), bf16[64,1,96]{2,1,0:T(2,128)(2,1)S(1)}, u32[]{:S(2)}, u32[]{:S(2)}) async-start(bf16[64,1,96]{2,1,0:T(2,128)(2,1)} %copy.18), calls=%async_computation.3 | async-start | bytes 65536 | tf_op jit(solution)/shard_map/all_to_all | solution.py:108
  135.6 4.8 %fusion.30 = f32[256,256]{1,0:T(8,128)S(1)} fusion(bf16[64,96,256]{2,1,0:T(8,128)(2,1)} %all-to-all-done.1, f32[64,96]{1,0:T(8,128)S(1)} %bitcast.89), kind=kOutput, calls=%fused_computation.34 | convolution fusion | flops 810024960 | bytes 3432448 | tf_op jit(solution)/shard_map/dot_general | solution.py:116
  140.4 1.2 broadcast_multiply_fusion
  141.6 2.7 %all-to-all-done.3 = bf16[64,1,96]{2,1,0:T(2,128)(2,1)S(1)} async-done(((bf16[64,1,96]{2,1,0:T(2,128)(2,1)}), bf16[64,1,96]{2,1,0:T(2,128)(2,1)S(1)}, u32[]{:S(2)}, u32[]{:S(2)}) %all-to-all-start.3) | async-done | bytes 12320 | tf_op jit(solution)/shard_map/all_to_all | solution.py:108
  144.2 4.5 %all-to-all-start.2 = ((f32[4,256,256]{2,1,0:T(8,128)}), f32[4,256,256]{2,1,0:T(8,128)}, u32[]{:S(2)}, u32[]{:S(2)}) async-start(f32[4,256,256]{2,1,0:T(8,128)} %broadcast_multiply_fusion), calls=%async_computation.2 | async-start | bytes 2097152 | tf_op jit(solution)/shard_map/all_to_all | solution.py:18
  148.7 2.6 %fusion.15 = f32[1,256,1]{1,0,2:T(1,128)S(1)} fusion(bf16[64,96,256]{2,1,0:T(8,128)(2,1)} %all-to-all-done.1, f32[64,96]{1,0:T(8,128)S(1)} %bitcast.90, bf16[64,1,96]{2,1,0:T(2,128)(2,1)S(1)} %all-to-all-done.3), kind=kOutput, calls=%fused_computation.17 | convolution fusion | flops 7864320 | bytes 3183616 | tf_op jit(solution)/shard_map/dot_general | solution.py:117
  151.4 14.7 %psum.7 = f32[4,256]{1,0:T(4,128)S(1)} all-reduce(f32[4,256]{1,0:T(4,128)S(1)} %broadcast_multiply_fusion.2), channel_id=1, replica_groups=mesh['region'=64,'level'=4] {'level'}, use_global_device_ids=true, to_apply=%region_4.5 | all-reduce | flops 1024 | bytes 8192 | tf_op jit(solution)/shard_map/psum | solution.py:124
  166.1 1.3 reduce_sum.27
  167.4 0.7 multiply_reduce_fusion
  169.2 0.4 fusion.40
  169.9 0.4 fusion.28
  170.2 0.4 fusion.78
  170.6 0.4 fusion.77
  171.0 0.4 fusion.27
  171.4 0.4 fusion.79
  171.8 0.4 fusion.80
  172.2 0.4 fusion.26
  172.6 0.4 convolution_divide_fusion
  173.6 2.2 %fusion.14 = bf16[1,256,4096]{2,1,0:T(8,128)(2,1)} fusion(bf16[1,256,4096]{2,1,0:T(8,128)(2,1)S(1)} %copy-done.1, f32[4096]{0:T(1024)S(1)} %broadcast_multiply_fusion.1, f32[256,256]{1,0:T(8,128)S(1)} %convolution_divide_fusion, f32[256]{0:T(256)S(1)} %bitcast.93), kind=kOutput, calls=%fused_computation.16 | convolution fusion | flops 542310400 | bytes 4473856 | tf_op jit(solution)/shard_map/dot_general | solution.py:59
  (29 shorter events, 2.4 us)
Async XLA Ops:
  0.0 38.9 %copy-start = (bf16[1,1024,256]{2,1,0:T(8,128)(2,1)S(1)}, bf16[1,1024,256]{2,1,0:T(8,128)(2,1)}, u32[]{:S(2)}) copy-start(bf16[1,1024,256]{2,1,0:T(8,128)(2,1)} %param.7) | copy-start | bytes 1572868
  26.9 20.6 %all-to-all-start = ((bf16[64,1,96]{2,1,0:T(2,128)(2,1)}), bf16[64,1,96]{2,1,0:T(2,128)(2,1)S(1)}, u32[]{:S(2)}, u32[]{:S(2)}) async-start(bf16[64,1,96]{2,1,0:T(2,128)(2,1)} %copy.17), calls=%async_computation | async-start | bytes 65536 | tf_op jit(solution)/shard_map/all_to_all | solution.py:107
  45.8 10.7 %copy-start.2 = (bf16[1,1024]{1,0:T(2,128)(2,1)S(1)}, bf16[1,1024]{1,0:T(2,128)(2,1)}, u32[]{:S(2)}) copy-start(bf16[1,1024]{1,0:T(2,128)(2,1)} %param.8) | copy-start | bytes 6148
  47.5 80.9 %all-to-all-start.1 = ((bf16[64,96,256]{2,1,0:T(8,128)(2,1)}), bf16[64,96,256]{2,1,0:T(8,128)(2,1)}, u32[]{:S(2)}, u32[]{:S(2)}) async-start(bf16[64,96,256]{2,1,0:T(8,128)(2,1)} %fusion.21), calls=%async_computation.1 | async-start | bytes 6291456 | tf_op jit(solution)/shard_map/all_to_all | solution.py:106
  56.5 5.3 %copy-start.1 = (bf16[1,256,4096]{2,1,0:T(8,128)(2,1)S(1)}, bf16[1,256,4096]{2,1,0:T(8,128)(2,1)}, u32[]{:S(2)}) copy-start(bf16[1,256,4096]{2,1,0:T(8,128)(2,1)} %param.6) | copy-start | bytes 6291460
  128.3 15.9 %all-to-all-start.3 = ((bf16[64,1,96]{2,1,0:T(2,128)(2,1)}), bf16[64,1,96]{2,1,0:T(2,128)(2,1)S(1)}, u32[]{:S(2)}, u32[]{:S(2)}) async-start(bf16[64,1,96]{2,1,0:T(2,128)(2,1)} %copy.18), calls=%async_computation.3 | async-start | bytes 65536 | tf_op jit(solution)/shard_map/all_to_all | solution.py:108
  144.2 21.9 %all-to-all-start.2 = ((f32[4,256,256]{2,1,0:T(8,128)}), f32[4,256,256]{2,1,0:T(8,128)}, u32[]{:S(2)}, u32[]{:S(2)}) async-start(f32[4,256,256]{2,1,0:T(8,128)} %broadcast_multiply_fusion), calls=%async_computation.2 | async-start | bytes 2097152 | tf_op jit(solution)/shard_map/all_to_all | solution.py:18
where the time goes:
time: 176 us
  waiting for transfers between devices  70.4 us (40%)
  starting transfers between devices  32.7 us (19%)
  matrix products  31.8 us (18%)
  other arithmetic  22.6 us (13%)
  blocking collectives  14.7 us (8%)
  local copies, waits for them, and re-layouts  2.54 us (1%)
    all_to_all x1, waiting for transfers between devices, body(): lax.all_to_all(send_rows, 'region', split_axis=0, concat_axis=0, tiled=True)  66.1 us
    another operation x2, other arithmetic  18 us
    psum x1, blocking collectives, body(): all_sums = lax.psum(sum_terms, 'level')  14.7 us
    all_to_all x1, starting transfers between devices, body(): lax.all_to_all(send_gain, 'region', split_axis=0, concat_axis=0, tiled=True)  12 us
    all_to_all x1, starting transfers between devices, body(): lax.all_to_all(send_rows, 'region', split_axis=0, concat_axis=0, tiled=True)  8.98 us
    all_to_all x1, starting transfers between devices, body(): lax.all_to_all(send_innov, 'region', split_axis=0, concat_axis=0, tiled=T...  7.27 us
    dot_general x1, matrix products, body(): jnp.einsum('rso,om->rsm', placement.astype(jnp.bfloat16), obs_anomaly[0],...  6.88 us
    dot_general x1, matrix products, body(): jnp.dot(weighted.T, routed_rows, preferred_element_type=jnp.float32)  4.79 us
  transfers between devices with their start and end apart: 4, of which 3 were waited for; matrix products, arithmetic and copies ran while one was open for 12% of the time, Pallas kernels for 0%

commit v1 on v0

--- a/solution.py
+++ b/solution.py
@@ -121,7 +121,7 @@
     covariance = sum_at_owner(factor[:, None] * stacked, "level", 0)
     level_ids = jnp.arange(levels, dtype=jnp.int32)
     sum_terms = level_factor(jnp.abs(level_ids - my_level), levels)[:, None] * own_sum[None, :]
-    all_sums = lax.psum(sum_terms, "level")
+    all_sums = jnp.sum(lax.all_gather(sum_terms, "level"), axis=0)
     innovation_sum = lax.dynamic_index_in_dim(all_sums, my_level, 0, keepdims=False)
     transform = analysis_weights(covariance, innovation_sum)
     return update_columns(ensemble[0], transform)[None]

time: 176 us -> 179 us (1.017)
  blocking collectives: 14.7 us -> 17.6 us
    all_gather x0 -> x1, blocking collectives: none -> 17.6 us  [body(): all_sums = jnp.sum(lax.all_gather(sum_terms, 'level'), axis=0)]
    psum x1 -> x0, blocking collectives: 14.7 us -> none  [body(): all_sums = lax.psum(sum_terms, 'level')]
where the time goes in v1:
time: 179 us
  waiting for transfers between devices  70.4 us (39%)
  starting transfers between devices  32.7 us (18%)
  matrix products  31.8 us (18%)
  other arithmetic  22.6 us (13%)
  blocking collectives  17.6 us (10%)
  local copies, waits for them, and re-layouts  2.54 us (1%)
    all_to_all x1, waiting for transfers between devices, body(): lax.all_to_all(send_rows, 'region', split_axis=0, concat_axis=0, tiled=True)  66.1 us
    another operation x2, other arithmetic  18 us
    all_gather x1, blocking collectives, body(): all_sums = jnp.sum(lax.all_gather(sum_terms, 'level'), axis=0)  17.6 us
    all_to_all x1, starting transfers between devices, body(): lax.all_to_all(send_gain, 'region', split_axis=0, concat_axis=0, tiled=True)  12 us
    all_to_all x1, starting transfers between devices, body(): lax.all_to_all(send_rows, 'region', split_axis=0, concat_axis=0, tiled=True)  8.98 us
    all_to_all x1, starting transfers between devices, body(): lax.all_to_all(send_innov, 'region', split_axis=0, concat_axis=0, tiled=T...  7.27 us
    dot_general x1, matrix products, body(): jnp.einsum('rso,om->rsm', placement.astype(jnp.bfloat16), obs_anomaly[0],...  6.88 us
    dot_general x1, matrix products, body(): jnp.dot(weighted.T, routed_rows, preferred_element_type=jnp.float32)  4.79 us
  transfers between devices with their start and end apart: 4, of which 3 were waited for; matrix products, arithmetic and copies ran while one was open for 12% of the time, Pallas kernels for 0%

profile of v1, /device:TPU:2, one launch (start us, length us, event | category | flops | bytes accessed | tf_op | source)
XLA Modules:
  0.0 178.7 jit_solution(3640902812553018815)
XLA Ops:
  0.0 0.8 slice_bitcast_fusion.2
  0.8 0.7 convert_element_type.111
  1.5 1.2 fusion.32
  2.9 18.0 %reduce-window.6 = s32[64,8,128]{2,1,0:T(8,128)S(1)} reduce-window(s32[64,8,128]{2,1,0:T(8,128)S(1)} %bitcast.82, s32[]{:T(128)} %constant.70.clone.1), window={size=1x1x128 pad=0_0x0_0x127_0}, to_apply=%region_0.0 | reduce-window | flops 8323072 | bytes 524292 | tf_op jit(solution)/shard_map/reduce-window
  21.5 4.8 %fusion.5 = f32[64,1,96]{2,1,0:T(1,128)S(1)} fusion(s32[64,1024]{1,0:T(8,128)S(1)} %bitcast.84, pred[64,1024]{1,0:T(8,128)(4,1)S(1)} %get-tuple-element.6, bf16[1024,64,1]{0,1,2:T(8,128)(2,1)S(1)} %fusion.37), kind=kOutput, calls=%fused_computation.4 | convolution fusion | flops 25165824 | bytes 483328 | tf_op jit(solution)/shard_map/rso,or->rs/dot_general | solution.py:99
  26.2 0.6 copy.17
  26.9 12.0 %all-to-all-start = ((bf16[64,1,96]{2,1,0:T(2,128)(2,1)}), bf16[64,1,96]{2,1,0:T(2,128)(2,1)S(1)}, u32[]{:S(2)}, u32[]{:S(2)}) async-start(bf16[64,1,96]{2,1,0:T(2,128)(2,1)} %copy.17), calls=%async_computation | async-start | bytes 65536 | tf_op jit(solution)/shard_map/all_to_all | solution.py:107
  38.9 6.9 %fusion.21 = bf16[64,96,256]{2,1,0:T(8,128)(2,1)} fusion(s32[64,1024]{1,0:T(8,128)S(1)} %bitcast.85, pred[64,1024]{1,0:T(8,128)(4,1)S(1)} %get-tuple-element.6, bf16[1,1024,256]{2,1,0:T(8,128)(2,1)S(1)} %copy-done), kind=kOutput, calls=%fused_computation.23 | convolution fusion | flops 3235381248 | bytes 3997696 | tf_op jit(solution)/shard_map/rso,om->rsm/dot_general | solution.py:93
  45.8 1.7 all-to-all-done
  47.5 9.0 %all-to-all-start.1 = ((bf16[64,96,256]{2,1,0:T(8,128)(2,1)}), bf16[64,96,256]{2,1,0:T(8,128)(2,1)}, u32[]{:S(2)}, u32[]{:S(2)}) async-start(bf16[64,96,256]{2,1,0:T(8,128)(2,1)} %fusion.21), calls=%async_computation.1 | async-start | bytes 6291456 | tf_op jit(solution)/shard_map/all_to_all | solution.py:106
  56.5 4.7 %fusion.1 = f32[1,64,96]{2,0,1:T(1,128)S(1)} fusion(s32[64,1024]{1,0:T(8,128)S(1)} %bitcast.86, pred[64,1024]{1,0:T(8,128)(4,1)S(1)} %get-tuple-element.6, bf16[1,1024]{1,0:T(2,128)(2,1)S(1)} %copy-done.2), kind=kOutput, calls=%fused_computation.2 | convolution fusion | flops 25165824 | bytes 354304 | tf_op jit(solution)/shard_map/rso,o->rs/dot_general | solution.py:102
  61.2 0.6 copy.18
  62.2 66.1 %all-to-all-done.1 = bf16[64,96,256]{2,1,0:T(8,128)(2,1)} async-done(((bf16[64,96,256]{2,1,0:T(8,128)(2,1)}), bf16[64,96,256]{2,1,0:T(8,128)(2,1)}, u32[]{:S(2)}, u32[]{:S(2)}) %all-to-all-start.1) | async-done | bytes 3145760 | tf_op jit(solution)/shard_map/all_to_all | solution.py:106
  128.3 7.3 %all-to-all-start.3 = ((bf16[64,1,96]{2,1,0:T(2,128)(2,1)}), bf16[64,1,96]{2,1,0:T(2,128)(2,1)S(1)}, u32[]{:S(2)}, u32[]{:S(2)}) async-start(bf16[64,1,96]{2,1,0:T(2,128)(2,1)} %copy.18), calls=%async_computation.3 | async-start | bytes 65536 | tf_op jit(solution)/shard_map/all_to_all | solution.py:108
  135.6 4.8 %fusion.30 = f32[256,256]{1,0:T(8,128)S(1)} fusion(bf16[64,96,256]{2,1,0:T(8,128)(2,1)} %all-to-all-done.1, f32[64,96]{1,0:T(8,128)S(1)} %bitcast.89), kind=kOutput, calls=%fused_computation.34 | convolution fusion | flops 810024960 | bytes 3432448 | tf_op jit(solution)/shard_map/dot_general | solution.py:116
  140.4 1.2 broadcast_multiply_fusion
  141.6 2.7 %all-to-all-done.3 = bf16[64,1,96]{2,1,0:T(2,128)(2,1)S(1)} async-done(((bf16[64,1,96]{2,1,0:T(2,128)(2,1)}), bf16[64,1,96]{2,1,0:T(2,128)(2,1)S(1)}, u32[]{:S(2)}, u32[]{:S(2)}) %all-to-all-start.3) | async-done | bytes 12320 | tf_op jit(solution)/shard_map/all_to_all | solution.py:108
  144.2 4.5 %all-to-all-start.2 = ((f32[4,256,256]{2,1,0:T(8,128)}), f32[4,256,256]{2,1,0:T(8,128)}, u32[]{:S(2)}, u32[]{:S(2)}) async-start(f32[4,256,256]{2,1,0:T(8,128)} %broadcast_multiply_fusion), calls=%async_computation.2 | async-start | bytes 2097152 | tf_op jit(solution)/shard_map/all_to_all | solution.py:18
  148.7 2.6 %fusion.15 = f32[1,256,1]{1,0,2:T(1,128)S(1)} fusion(bf16[64,96,256]{2,1,0:T(8,128)(2,1)} %all-to-all-done.1, f32[64,96]{1,0:T(8,128)S(1)} %bitcast.90, bf16[64,1,96]{2,1,0:T(2,128)(2,1)S(1)} %all-to-all-done.3), kind=kOutput, calls=%fused_computation.17 | convolution fusion | flops 7864320 | bytes 3183616 | tf_op jit(solution)/shard_map/dot_general | solution.py:117
  151.4 17.6 %all_gather.4 = f32[4,4,256]{2,1,0:T(4,128)S(1)} all-gather(f32[1,4,256]{2,1,0:T(4,128)S(1)} %broadcast_multiply_fusion.2), channel_id=1, replica_groups=mesh['region'=64,'level'=4] {'level'}, dimensions={0}, use_global_device_ids=true | all-gather | bytes 20480 | tf_op jit(solution)/shard_map/all_gather | solution.py:124
  169.0 1.3 reduce_sum.36
  170.4 0.7 multiply_reduce_fusion
  172.1 0.4 fusion.40
  172.8 0.4 fusion.28
  173.2 0.4 fusion.78
  173.6 0.4 fusion.77
  174.0 0.4 fusion.27
  174.4 0.4 fusion.79
  174.7 0.4 fusion.80
  175.1 0.4 fusion.26
  175.5 0.4 convolution_divide_fusion
  176.5 2.2 %fusion.14 = bf16[1,256,4096]{2,1,0:T(8,128)(2,1)} fusion(bf16[1,256,4096]{2,1,0:T(8,128)(2,1)S(1)} %copy-done.1, f32[4096]{0:T(1024)S(1)} %broadcast_multiply_fusion.1, f32[256,256]{1,0:T(8,128)S(1)} %convolution_divide_fusion, f32[256]{0:T(256)S(1)} %bitcast.93), kind=kOutput, calls=%fused_computation.16 | convolution fusion | flops 542310400 | bytes 4473856 | tf_op jit(solution)/shard_map/dot_general | solution.py:59
  (30 shorter events, 2.4 us)
Async XLA Ops:
  0.0 38.9 %copy-start = (bf16[1,1024,256]{2,1,0:T(8,128)(2,1)S(1)}, bf16[1,1024,256]{2,1,0:T(8,128)(2,1)}, u32[]{:S(2)}) copy-start(bf16[1,1024,256]{2,1,0:T(8,128)(2,1)} %param.7) | copy-start | bytes 1572868
  26.9 20.6 %all-to-all-start = ((bf16[64,1,96]{2,1,0:T(2,128)(2,1)}), bf16[64,1,96]{2,1,0:T(2,128)(2,1)S(1)}, u32[]{:S(2)}, u32[]{:S(2)}) async-start(bf16[64,1,96]{2,1,0:T(2,128)(2,1)} %copy.17), calls=%async_computation | async-start | bytes 65536 | tf_op jit(solution)/shard_map/all_to_all | solution.py:107
  45.8 10.7 %copy-start.2 = (bf16[1,1024]{1,0:T(2,128)(2,1)S(1)}, bf16[1,1024]{1,0:T(2,128)(2,1)}, u32[]{:S(2)}) copy-start(bf16[1,1024]{1,0:T(2,128)(2,1)} %param.8) | copy-start | bytes 6148
  47.5 80.9 %all-to-all-start.1 = ((bf16[64,96,256]{2,1,0:T(8,128)(2,1)}), bf16[64,96,256]{2,1,0:T(8,128)(2,1)}, u32[]{:S(2)}, u32[]{:S(2)}) async-start(bf16[64,96,256]{2,1,0:T(8,128)(2,1)} %fusion.21), calls=%async_computation.1 | async-start | bytes 6291456 | tf_op jit(solution)/shard_map/all_to_all | solution.py:106
  56.5 5.3 %copy-start.1 = (bf16[1,256,4096]{2,1,0:T(8,128)(2,1)S(1)}, bf16[1,256,4096]{2,1,0:T(8,128)(2,1)}, u32[]{:S(2)}) copy-start(bf16[1,256,4096]{2,1,0:T(8,128)(2,1)} %param.6) | copy-start | bytes 6291460
  128.3 15.9 %all-to-all-start.3 = ((bf16[64,1,96]{2,1,0:T(2,128)(2,1)}), bf16[64,1,96]{2,1,0:T(2,128)(2,1)S(1)}, u32[]{:S(2)}, u32[]{:S(2)}) async-start(bf16[64,1,96]{2,1,0:T(2,128)(2,1)} %copy.18), calls=%async_computation.3 | async-start | bytes 65536 | tf_op jit(solution)/shard_map/all_to_all | solution.py:108
  144.2 24.8 %all-to-all-start.2 = ((f32[4,256,256]{2,1,0:T(8,128)}), f32[4,256,256]{2,1,0:T(8,128)}, u32[]{:S(2)}, u32[]{:S(2)}) async-start(f32[4,256,256]{2,1,0:T(8,128)} %broadcast_multiply_fusion), calls=%async_computation.2 | async-start | bytes 2097152 | tf_op jit(solution)/shard_map/all_to_all | solution.py:18
